TPU v7x, 256 devices: a whole 4x4x8 slice. The times are simulated.
256 devices in a mesh: layer: 4 (over x), row: 8 (over y, core), col: 8 (over z).
Axes of the slice: x: 4, y: 4, z: 8, core: 2. Of those that a mesh axis runs over, the one named last changes fastest.
Arguments:
- left_values: bfloat16 [8192, 4, 2048], P('row', 'layer', 'col'), may hold values from -22 to 22
- left_pattern: int32 [32, 4, 8], P('row', 'layer', 'col'), may hold values from 0 to 1, as said below
- right_values: bfloat16 [8192, 4, 2048], P(('layer', 'row'), None, 'col'), may hold values from -6 to 6
- right_pattern: int32 [32, 4, 8], P(('layer', 'row'), None, 'col'), may hold values from 0 to 1, as said below
Outputs:
- expanded: bfloat16 [8192, 4, 2048], P('row', 'layer', 'col')
Inputs may be any that keep to these rules, and one draw needn't show every extreme that they name: `left_pattern`: 1 marks a stored tile, 0 an absent one. `right_pattern`: 1 marks a stored tile, 0 an absent one.
All inputs are finite; a program needn't handle non-finite values.
Results may differ from a plain program's by a relative error of at most 0.001.
Values may be sent and summed in bfloat16 or wider, within the bound.
A program may use at most 64 MiB of HBM per device.

v0:
```python
import jax
import jax.numpy as jnp
from jax import lax
from jax.sharding import PartitionSpec as P


def expand_tiles(values, pattern):
    tile_rows, layers, tile_cols = pattern.shape
    tile_size = values.shape[0] // tile_rows
    blocks = values.reshape(tile_rows, tile_size, layers, tile_cols, tile_size)
    blocks = blocks * pattern[:, None, :, :, None].astype(values.dtype)
    return blocks.reshape(values.shape)


def per_device(left_values, left_pattern, right_values, right_pattern):
    left_block = expand_tiles(left_values, left_pattern)
    right_block = expand_tiles(right_values, right_pattern)
    rows_local = left_block.shape[0]
    columns_local = left_block.shape[2]
    left_flat = left_block.reshape(rows_local, columns_local)
    right_flat = right_block.reshape(right_block.shape[0], -1)
    right_all = lax.all_gather(right_flat, "row", axis=0, tiled=True)
    left_all = lax.all_gather(left_flat, "col", axis=1, tiled=True)
    partial = jnp.dot(left_all, right_all, preferred_element_type=jnp.float32)
    layers = lax.axis_size("layer")
    partial = jnp.stack(
        [partial[:, columns_local * l : columns_local * (l + 1)] for l in range(layers)], axis=0
    )
    product = lax.psum_scatter(partial, "layer", scatter_dimension=0, tiled=True)
    product = product.reshape(rows_local, 1, columns_local)
    squared = product * product
    column = lax.psum(jnp.sum(squared, axis=0, keepdims=True), "row")
    rows_total = rows_local * lax.axis_size("row")
    colmean = column / rows_total
    return (squared / (colmean + 1e-06)).astype(jnp.bfloat16)


def solution(mesh):
    return jax.shard_map(
        per_device,
        mesh=mesh,
        in_specs=(
            P("row", "layer", "col"),
            P("row", "layer", "col"),
            P(("layer", "row"), None, "col"),
            P(("layer", "row"), None, "col"),
        ),
        out_specs=P("row", "layer", "col"),
        check_vma=False,
    )
```

profile of v0, /device:TPU:32, one launch (start us, length us, event | category | flops | bytes accessed | tf_op | source)
XLA Modules:
  0.0 194.0 jit_solution(14705510479955236059)
XLA Ops:
  6.5 0.0 all-gather.3.cloned.1.call-start
  6.5 0.7 convert_bitcast_fusion.1
  7.2 0.1 broadcast_bitcast_fusion
  7.3 2.0 %bitcast_multiply_fusion = bf16[1024,256]{1,0:T(8,128)(2,1)} fusion(bf16[1024,1,256]{2,0,1:T(8,128)(2,1)} %param.4, bf16[1024]{0:T(1024)(128)(2,1)S(1)} %bitcast.29), kind=kLoop, calls=%fused_computation.8 | loop fusion | flops 262144 | bytes 1050624 | tf_op jit(solution)/shard_map/mul | solution.py:11
  9.3 0.0 all-gather.3.cloned.1.call-update
  9.3 0.0 all-gather.5.cloned.1.call-start
  9.4 0.7 convert_bitcast_fusion
  10.1 1.3 broadcast_multiply_fusion
  11.4 0.9 copy.6
  12.3 0.0 all-gather.5.cloned.1.call-update
  12.4 0.0 reduce-scatter.2.cloned.1.call-start
  12.4 62.3 %all-gather.3.cloned.1.call-done = bf16[1024,2048]{1,0:T(8,128)(2,1)} async-done(((bf16[1024,256]{1,0:T(8,128)(2,1)}), bf16[1024,2048]{1,0:T(8,128)(2,1)}) %all-gather.3.cloned.1.call-update) | async-done | bytes 4194320 | tf_op jit(solution)/shard_map/all_gather | solution.py:23
  74.7 35.0 %all-gather.5.cloned.1.call-done = bf16[2048,1024]{1,0:T(8,128)(2,1)} async-done(((bf16[256,1024]{1,0:T(8,128)(2,1)}), bf16[2048,1024]{1,0:T(8,128)(2,1)}) %all-gather.5.cloned.1.call-update) | async-done | bytes 4194320 | tf_op jit(solution)/shard_map/all_gather | solution.py:22
  109.7 7.5 %fusion.1 = f32[1024,1024]{1,0:T(8,128)S(1)} fusion(bf16[1024,2048]{1,0:T(8,128)(2,1)} %all-gather.3.cloned.1.call-done, bf16[2048,1024]{1,0:T(8,128)(2,1)} %all-gather.5.cloned.1.call-done), kind=kOutput, calls=%fused_computation.14 | convolution fusion | flops 4294967296 | bytes 12582912 | tf_op jit(solution)/shard_map/dot_general | solution.py:24
  117.2 0.4 slice_bitcast_fusion.3
  117.6 2.2 %pad_maximum_fusion = f32[4,1024,256]{2,1,0:T(8,128)} fusion(f32[1,1024,256]{2,1,0:T(8,128)S(1)} %get-tuple-element.6, f32[1,1024,256]{2,1,0:T(8,128)S(1)} %get-tuple-element.7, f32[1,1024,256]{2,1,0:T(8,128)S(1)} %get-tuple-element.8, f32[1,1024,256]{2,1,0:T(8,128)S(1)} %get-tuple-element.5), kind=kLoop, calls=%fused_computation | loop fusion | flops 3145728 | bytes 8388608 | tf_op jit(solution)/shard_map/stack | solution.py:26
  119.8 0.0 reduce-scatter.2.cloned.1.call-update
  119.8 49.5 %reduce-scatter.2.cloned.1.call-done = f32[1,1024,256]{2,1,0:T(8,128)} async-done(((f32[4,1024,256]{2,1,0:T(8,128)}), f32[1,1024,256]{2,1,0:T(8,128)}) %reduce-scatter.2.cloned.1.call-update) | async-done | bytes 1048592 | tf_op jit(solution)/shard_map/reduce_scatter | solution.py:29
  169.3 1.4 multiply_reduce_fusion
  170.7 14.6 %psum.7 = f32[1,1,256]{2,1,0:T(1,128)S(1)} all-reduce(f32[1,1,256]{2,1,0:T(1,128)S(1)} %bitcast.30), channel_id=1, replica_groups=mesh['layer'=4,'row'=8,'col'=8] {'row'}, use_global_device_ids=true, to_apply=%region_2.0 | all-reduce | flops 256 | bytes 2048 | tf_op jit(solution)/shard_map/psum | solution.py:32
  185.3 2.1 %fusion = bf16[1024,1,256]{2,0,1:T(8,128)(2,1)} fusion(f32[1,1024,256]{2,1,0:T(8,128)} %reduce-scatter.2.cloned.1.call-done, f32[256]{0:T(256)S(1)} %bitcast.31), kind=kLoop, calls=%fused_computation.6 | loop fusion | flops 786432 | bytes 1573888 | tf_op jit(solution)/shard_map/convert_element_type | solution.py:35
  (2 shorter events, 0.0 us)
Async XLA Ops:
  6.5 68.1 %all-gather.3.cloned.1.call-start = ((), (), s32[]{:S(2)}) async-start(), calls=%async_computation.1 | async-start | bytes 4718592 | tf_op jit(solution)/shard_map/all_gather | solution.py:23
  9.3 100.4 %all-gather.5.cloned.1.call-start = ((), (), s32[]{:S(2)}) async-start(), calls=%async_computation.2 | async-start | bytes 4718592 | tf_op jit(solution)/shard_map/all_gather | solution.py:22
  12.4 156.9 %reduce-scatter.2.cloned.1.call-start = ((), (), s32[]{:S(2)}) async-start(), calls=%async_computation.3 | async-start | bytes 5242880 | tf_op jit(solution)/shard_map/reduce_scatter | solution.py:29
Sparse Core Ops, SparseCore 0:
  9.5 65.1 all-gather.2
  76.5 33.1 all-gather.4
  120.0 49.2 reduce-scatter.1
where the time goes:
time: 194 us
  waiting for transfers between devices  147 us (76%)
  blocking collectives  14.6 us (8%)
  between operations  13.1 us (7%)
  other arithmetic  10.4 us (5%)
  matrix products  7.5 us (4%)
    all_gather x1, waiting for transfers between devices, per_device(): left_all = lax.all_gather(left_flat, 'col', axis=1, tiled=True)  62.3 us
    reduce_scatter x1, waiting for transfers between devices, per_device(): lax.psum_scatter(partial, 'layer', scatter_dimension=0, tiled=True)  49.5 us
    all_gather x1, waiting for transfers between devices, per_device(): right_all = lax.all_gather(right_flat, 'row', axis=0, tiled=True)  35 us
    psum x1, blocking collectives, per_device(): column = lax.psum(jnp.sum(squared, axis=0, keepdims=True), 'row')  14.6 us
    dot_general x1, matrix products, per_device(): partial = jnp.dot(left_all, right_all, preferred_element_type=jnp.float32)  7.5 us
  transfers between devices with their start and end apart: 3, of which 3 were waited for; matrix products, arithmetic and copies ran while one was open for 2% of the time, Pallas kernels for 0%

commit v1 on v0

--- a/solution.py
+++ b/solution.py
@@ -2,6 +2,22 @@
 import jax.numpy as jnp
 from jax import lax
 from jax.sharding import PartitionSpec as P
+
+
+def flows_store(buf, chip_axis):
+    workers = lax.psum(1, chip_axis)
+    spare = range(1, workers)
+    mid_arr = map(lambda t: (t - 1, t), spare)
+    outer = list(mid_arr)
+    taken_in = outer + [(workers - 1, 0)]
+    q_next = buf
+    pool = [q_next]
+    for _ in range(workers - 1):
+        q_next = lax.ppermute(q_next, chip_axis, taken_in)
+        pool += [q_next]
+    left_arr = jnp.concatenate([*reversed(pool)], 0)
+    carry_out = lax.axis_index(chip_axis)
+    return jnp.roll(left_arr, (carry_out + 1) * q_next.shape[0], 0)
 
 
 def expand_tiles(values, pattern):
@@ -19,7 +35,7 @@
     columns_local = left_block.shape[2]
     left_flat = left_block.reshape(rows_local, columns_local)
     right_flat = right_block.reshape(right_block.shape[0], -1)
-    right_all = lax.all_gather(right_flat, "row", axis=0, tiled=True)
+    right_all = flows_store(right_flat, "row")
     left_all = lax.all_gather(left_flat, "col", axis=1, tiled=True)
     partial = jnp.dot(left_all, right_all, preferred_element_type=jnp.float32)
     layers = lax.axis_size("layer")

time: 194 us -> 183 us (0.943)
  waiting for transfers between devices: 147 us -> 119 us
  local copies, waits for them, and re-layouts: 1.42 us -> 18.1 us
    ppermute x0 -> x7, waiting for transfers between devices: none -> 69.1 us  [flows_store(): q_next = lax.ppermute(q_next, chip_axis, taken_in)]
    all_gather x1, waiting for transfers between devices: 62.3 us -> 0.01 us  [per_device(): left_all = lax.all_gather(left_flat, 'col', axis=1, tiled=True)]
    all_gather x1 -> x0, waiting for transfers between devices: 35 us -> none  [per_device(): right_all = lax.all_gather(right_flat, 'row', axis=0, tiled=True)]
    unnamed x3 -> x18, local copies, waits for them, and re-layouts: 1.03 us -> 16.8 us
  transfers between devices with their start and end apart: 3 -> 9, of which waited for: 3 -> 8; matrix products, arithmetic and copies ran while one was open for 2% -> 11% of each run, Pallas kernels for 0% -> 0%
where the time goes in v1:
time: 183 us
  waiting for transfers between devices  119 us (65%)
  local copies, waits for them, and re-layouts  18.1 us (10%)
  blocking collectives  14.6 us (8%)
  between operations  13.5 us (7%)
  other arithmetic  10.4 us (6%)
  matrix products  7.51 us (4%)
    ppermute x7, waiting for transfers between devices, flows_store(): q_next = lax.ppermute(q_next, chip_axis, taken_in)  69.1 us
    reduce_scatter x1, waiting for transfers between devices, per_device(): lax.psum_scatter(partial, 'layer', scatter_dimension=0, tiled=True)  49.5 us
    unnamed x18, local copies, waits for them, and re-layouts  16.8 us
    psum x1, blocking collectives, per_device(): column = lax.psum(jnp.sum(squared, axis=0, keepdims=True), 'row')  14.6 us
    dot_general x1, matrix products, per_device(): partial = jnp.dot(left_all, right_all, preferred_element_type=jnp.float32)  7.51 us
  transfers between devices with their start and end apart: 9, of which 8 were waited for; matrix products, arithmetic and copies ran while one was open for 11% of the time, Pallas kernels for 0%

profile of v1, /device:TPU:32, one launch (start us, length us, event | category | flops | bytes accessed | tf_op | source)
XLA Modules:
  0.0 182.7 jit_solution(17738077982640674386)
XLA Ops:
  6.5 0.0 all-gather.2.cloned.1.call-start
  6.5 0.7 convert_bitcast_fusion.1
  7.2 0.1 broadcast_bitcast_fusion
  7.3 2.0 %bitcast_multiply_fusion = bf16[1024,256]{1,0:T(8,128)(2,1)} fusion(bf16[1024,1,256]{2,0,1:T(8,128)(2,1)} %param.4, bf16[1024]{0:T(1024)(128)(2,1)S(1)} %bitcast.30), kind=kLoop, calls=%fused_computation.10 | loop fusion | flops 262144 | bytes 1050624 | tf_op jit(solution)/shard_map/mul | solution.py:27
  9.3 0.0 all-gather.2.cloned.1.call-update
  9.3 0.0 reduce-scatter.2.cloned.1.call-start
  9.4 0.7 convert_bitcast_fusion
  10.1 1.3 broadcast_multiply_fusion
  11.4 0.1 copy.6
  11.5 0.0 collective-permute-start
  11.5 9.8 %collective-permute-done = bf16[256,1024]{1,0:T(8,128)(2,1)S(1)} collective-permute-done((bf16[256,1024]{1,0:T(8,128)(2,1)S(1)}, bf16[256,1024]{1,0:T(8,128)(2,1)S(1)}, u32[]{:S(2)}, u32[]{:S(2)}) %collective-permute-start) | collective-permute-done | bytes 524320 | tf_op jit(solution)/shard_map/ppermute | solution.py:16
  21.3 0.0 collective-permute-start.1
  21.3 9.8 %collective-permute-done.1 = bf16[256,1024]{1,0:T(8,128)(2,1)S(1)} collective-permute-done((bf16[256,1024]{1,0:T(8,128)(2,1)S(1)}, bf16[256,1024]{1,0:T(8,128)(2,1)S(1)}, u32[]{:S(2)}, u32[]{:S(2)}) %collective-permute-start.1) | collective-permute-done | bytes 524320 | tf_op jit(solution)/shard_map/ppermute | solution.py:16
  31.1 0.0 collective-permute-start.2
  31.1 9.8 %collective-permute-done.2 = bf16[256,1024]{1,0:T(8,128)(2,1)S(1)} collective-permute-done((bf16[256,1024]{1,0:T(8,128)(2,1)S(1)}, bf16[256,1024]{1,0:T(8,128)(2,1)S(1)}, u32[]{:S(2)}, u32[]{:S(2)}) %collective-permute-start.2) | collective-permute-done | bytes 524320 | tf_op jit(solution)/shard_map/ppermute | solution.py:16
  41.0 0.0 collective-permute-start.3
  41.0 9.8 %collective-permute-done.3 = bf16[256,1024]{1,0:T(8,128)(2,1)S(1)} collective-permute-done((bf16[256,1024]{1,0:T(8,128)(2,1)S(1)}, bf16[256,1024]{1,0:T(8,128)(2,1)S(1)}, u32[]{:S(2)}, u32[]{:S(2)}) %collective-permute-start.3) | collective-permute-done | bytes 524320 | tf_op jit(solution)/shard_map/ppermute | solution.py:16
  50.8 0.0 collective-permute-start.4
  50.8 9.8 %collective-permute-done.4 = bf16[256,1024]{1,0:T(8,128)(2,1)S(1)} collective-permute-done((bf16[256,1024]{1,0:T(8,128)(2,1)S(1)}, bf16[256,1024]{1,0:T(8,128)(2,1)S(1)}, u32[]{:S(2)}, u32[]{:S(2)}) %collective-permute-start.4) | collective-permute-done | bytes 524320 | tf_op jit(solution)/shard_map/ppermute | solution.py:16
  60.6 0.0 collective-permute-start.5
  60.6 9.9 %collective-permute-done.5 = bf16[256,1024]{1,0:T(8,128)(2,1)} collective-permute-done((bf16[256,1024]{1,0:T(8,128)(2,1)S(1)}, bf16[256,1024]{1,0:T(8,128)(2,1)}, u32[]{:S(2)}, u32[]{:S(2)}) %collective-permute-start.5) | collective-permute-done | bytes 524320 | tf_op jit(solution)/shard_map/ppermute | solution.py:16
  70.5 0.0 collective-permute-start.6
  70.5 10.1 %collective-permute-done.6 = bf16[256,1024]{1,0:T(8,128)(2,1)} collective-permute-done((bf16[256,1024]{1,0:T(8,128)(2,1)}, bf16[256,1024]{1,0:T(8,128)(2,1)}, u32[]{:S(2)}, u32[]{:S(2)}) %collective-permute-start.6) | collective-permute-done | bytes 524320 | tf_op jit(solution)/shard_map/ppermute | solution.py:16
  80.6 1.9 %constant_dynamic-update-slice_fusion.15 = bf16[4096,1024]{1,0:T(8,128)(2,1)} fusion(bf16[256,1024]{1,0:T(8,128)(2,1)} %collective-permute-done.6), kind=kLoop, calls=%fused_computation.27 | loop fusion | bytes 1048576
  82.5 1.9 %constant_dynamic-update-slice_fusion.14 = bf16[4096,1024]{1,0:T(8,128)(2,1)} fusion(bf16[4096,1024]{1,0:T(8,128)(2,1)} %constant_dynamic-update-slice_fusion.15, bf16[256,1024]{1,0:T(8,128)(2,1)} %collective-permute-done.5), kind=kLoop, calls=%fused_computation.26 | loop fusion | bytes 1048576
  84.4 0.8 constant_dynamic-update-slice_fusion.13
  85.2 0.8 constant_dynamic-update-slice_fusion.12
  86.0 0.8 constant_dynamic-update-slice_fusion.11
  86.9 0.8 constant_dynamic-update-slice_fusion.10
  87.7 0.8 constant_dynamic-update-slice_fusion.9
  88.5 0.8 constant_dynamic-update-slice_fusion.8
  89.4 1.9 %constant_dynamic-update-slice_fusion.7 = bf16[4096,1024]{1,0:T(8,128)(2,1)} fusion(bf16[4096,1024]{1,0:T(8,128)(2,1)} %constant_dynamic-update-slice_fusion.8, bf16[256,1024]{1,0:T(8,128)(2,1)} %collective-permute-done.6), kind=kLoop, calls=%fused_computation.19 | loop fusion | bytes 1048576
  91.2 1.9 %constant_dynamic-update-slice_fusion.6 = bf16[4096,1024]{1,0:T(8,128)(2,1)} fusion(bf16[4096,1024]{1,0:T(8,128)(2,1)} %constant_dynamic-update-slice_fusion.7, bf16[256,1024]{1,0:T(8,128)(2,1)} %collective-permute-done.5), kind=kLoop, calls=%fused_computation.18 | loop fusion | bytes 1048576
  93.1 0.8 constant_dynamic-update-slice_fusion.5
  94.0 0.8 constant_dynamic-update-slice_fusion.4
  94.8 0.8 constant_dynamic-update-slice_fusion.3
  95.6 0.8 constant_dynamic-update-slice_fusion.2
  96.5 0.8 constant_dynamic-update-slice_fusion.1
  97.3 0.9 constant_dynamic-update-slice_fusion
  98.1 0.0 all-gather.2.cloned.1.call-done
  98.1 7.5 %fusion = f32[1024,1024]{1,0:T(8,128)S(1)} fusion(bf16[1024,2048]{1,0:T(8,128)(2,1)} %all-gather.2.cloned.1.call-done, bf16[4096,1024]{1,0:T(8,128)(2,1)} %constant_dynamic-update-slice_fusion, s32[]{:T(128)S(6)} %select_n.14), kind=kOutput, calls=%fused_computation.1 | convolution fusion | flops 4294967296 | bytes 12582916 | tf_op jit(solution)/shard_map/dot_general | solution.py:40
  105.7 0.4 slice_bitcast_fusion.3
  106.1 2.2 %pad_maximum_fusion = f32[4,1024,256]{2,1,0:T(8,128)} fusion(f32[1,1024,256]{2,1,0:T(8,128)S(1)} %get-tuple-element.6, f32[1,1024,256]{2,1,0:T(8,128)S(1)} %get-tuple-element.7, f32[1,1024,256]{2,1,0:T(8,128)S(1)} %get-tuple-element.8, f32[1,1024,256]{2,1,0:T(8,128)S(1)} %get-tuple-element.5), kind=kLoop, calls=%fused_computation | loop fusion | flops 3145728 | bytes 8388608 | tf_op jit(solution)/shard_map/stack | solution.py:42
  108.3 0.0 reduce-scatter.2.cloned.1.call-update
  108.3 49.5 %reduce-scatter.2.cloned.1.call-done = f32[1,1024,256]{2,1,0:T(8,128)} async-done(((f32[4,1024,256]{2,1,0:T(8,128)}), f32[1,1024,256]{2,1,0:T(8,128)}) %reduce-scatter.2.cloned.1.call-update) | async-done | bytes 1048592 | tf_op jit(solution)/shard_map/reduce_scatter | solution.py:45
  157.7 1.4 multiply_reduce_fusion
  159.1 14.6 %psum.7 = f32[1,1,256]{2,1,0:T(1,128)S(1)} all-reduce(f32[1,1,256]{2,1,0:T(1,128)S(1)} %bitcast.31), channel_id=1, replica_groups=mesh['layer'=4,'row'=8,'col'=8] {'row'}, use_global_device_ids=true, to_apply=%region_2.3 | all-reduce | flops 256 | bytes 2048 | tf_op jit(solution)/shard_map/psum | solution.py:48
  173.8 2.1 %fusion.2 = bf16[1024,1,256]{2,0,1:T(8,128)(2,1)} fusion(f32[1,1024,256]{2,1,0:T(8,128)} %reduce-scatter.2.cloned.1.call-done, f32[256]{0:T(256)S(1)} %bitcast.32), kind=kLoop, calls=%fused_computation.8 | loop fusion | flops 786432 | bytes 1573888 | tf_op jit(solution)/shard_map/convert_element_type | solution.py:51
  (2 shorter events, 0.0 us)
Async XLA Ops:
  6.5 91.6 %all-gather.2.cloned.1.call-start = ((), (), s32[]{:S(2)}) async-start(), calls=%async_computation.1 | async-start | bytes 4718592 | tf_op jit(solution)/shard_map/all_gather | solution.py:39
  9.3 148.4 %reduce-scatter.2.cloned.1.call-start = ((), (), s32[]{:S(2)}) async-start(), calls=%async_computation.2 | async-start | bytes 5242880 | tf_op jit(solution)/shard_map/reduce_scatter | solution.py:45
  11.5 9.8 %collective-permute-start = (bf16[256,1024]{1,0:T(8,128)(2,1)S(1)}, bf16[256,1024]{1,0:T(8,128)(2,1)S(1)}, u32[]{:S(2)}, u32[]{:S(2)}) collective-permute-start(bf16[256,1024]{1,0:T(8,128)(2,1)S(1)} %bitcast.26), channel_id=1, source_target_pairs={{0,8},{8,16},{16,24},{24,32},{32,40},{40,48},{48,56},{56,0},{1,9},... | collective-permute-start | bytes 1572872 | tf_op jit(solution)/shard_map/ppermute | solution.py:16
  21.3 9.8 %collective-permute-start.1 = (bf16[256,1024]{1,0:T(8,128)(2,1)S(1)}, bf16[256,1024]{1,0:T(8,128)(2,1)S(1)}, u32[]{:S(2)}, u32[]{:S(2)}) collective-permute-start(bf16[256,1024]{1,0:T(8,128)(2,1)S(1)} %collective-permute-done), channel_id=1, source_target_pairs={{0,8},{8,16},{16,24},{24,32},{32,40},{40,48},{48,56},{56,0},{1,9},... | collective-permute-start | bytes 1572872 | tf_op jit(solution)/shard_map/ppermute | solution.py:16
  31.1 9.8 %collective-permute-start.2 = (bf16[256,1024]{1,0:T(8,128)(2,1)S(1)}, bf16[256,1024]{1,0:T(8,128)(2,1)S(1)}, u32[]{:S(2)}, u32[]{:S(2)}) collective-permute-start(bf16[256,1024]{1,0:T(8,128)(2,1)S(1)} %collective-permute-done.1), channel_id=1, source_target_pairs={{0,8},{8,16},{16,24},{24,32},{32,40},{40,48},{48,56},{56,0},{1,9},... | collective-permute-start | bytes 1572872 | tf_op jit(solution)/shard_map/ppermute | solution.py:16
  41.0 9.8 %collective-permute-start.3 = (bf16[256,1024]{1,0:T(8,128)(2,1)S(1)}, bf16[256,1024]{1,0:T(8,128)(2,1)S(1)}, u32[]{:S(2)}, u32[]{:S(2)}) collective-permute-start(bf16[256,1024]{1,0:T(8,128)(2,1)S(1)} %collective-permute-done.2), channel_id=1, source_target_pairs={{0,8},{8,16},{16,24},{24,32},{32,40},{40,48},{48,56},{56,0},{1,9},... | collective-permute-start | bytes 1572872 | tf_op jit(solution)/shard_map/ppermute | solution.py:16
  50.8 9.8 %collective-permute-start.4 = (bf16[256,1024]{1,0:T(8,128)(2,1)S(1)}, bf16[256,1024]{1,0:T(8,128)(2,1)S(1)}, u32[]{:S(2)}, u32[]{:S(2)}) collective-permute-start(bf16[256,1024]{1,0:T(8,128)(2,1)S(1)} %collective-permute-done.3), channel_id=1, source_target_pairs={{0,8},{8,16},{16,24},{24,32},{32,40},{40,48},{48,56},{56,0},{1,9},... | collective-permute-start | bytes 1572872 | tf_op jit(solution)/shard_map/ppermute | solution.py:16
  60.6 9.9 %collective-permute-start.5 = (bf16[256,1024]{1,0:T(8,128)(2,1)S(1)}, bf16[256,1024]{1,0:T(8,128)(2,1)}, u32[]{:S(2)}, u32[]{:S(2)}) collective-permute-start(bf16[256,1024]{1,0:T(8,128)(2,1)S(1)} %collective-permute-done.4), channel_id=1, source_target_pairs={{0,8},{8,16},{16,24},{24,32},{32,40},{40,48},{48,56},{56,0},{1,9},... | collective-permute-start | bytes 1572872 | tf_op jit(solution)/shard_map/ppermute | solution.py:16
  70.5 10.1 %collective-permute-start.6 = (bf16[256,1024]{1,0:T(8,128)(2,1)}, bf16[256,1024]{1,0:T(8,128)(2,1)}, u32[]{:S(2)}, u32[]{:S(2)}) collective-permute-start(bf16[256,1024]{1,0:T(8,128)(2,1)} %collective-permute-done.5), channel_id=1, source_target_pairs={{0,8},{8,16},{16,24},{24,32},{32,40},{40,48},{48,56},{56,0},{1,9},... | collective-permute-start | bytes 1572872 | tf_op jit(solution)/shard_map/ppermute | solution.py:16
Sparse Core Ops, SparseCore 0:
  9.5 64.9 all-gather.1
  108.4 49.2 reduce-scatter.1
